TPU v7x, 512 devices: a whole 4x4x16 slice. The times are simulated.
512 devices in a mesh: visit: 64 (over z, y), template: 8 (over x, core).
Axes of the slice: x: 4, y: 4, z: 16, core: 2. Of those that a mesh axis runs over, the one named last changes fastest.
Arguments:
- template: bfloat16 [64, 256, 1152], P('visit', 'template'), may hold values from -5 to 5
- science: bfloat16 [384, 4, 256, 128], P('visit', None, 'template'), may hold values from -27 to 27
- variance: bfloat16 [384, 4, 256, 128], P('visit', None, 'template'), may hold values from 0.5 to 2
- bad_pixels: int32 [384, 4, 256, 128], P('visit', None, 'template'), may hold values 0 or 1
- intersection_patch: int32 [384, 4], P('visit'), may hold values from 0 to 63, as said below
- intersection_block: int32 [384, 4], P('visit'), may hold values from 0 to 7
Outputs:
- significance: float32 [64, 256, 1024], P('visit', 'template')
Inputs may be any that keep to these rules, and one draw needn't show every extreme that they name: `intersection_patch`: each visit's 4 patches are different. Among the 6 visits of one index of visit (an aligned block of rows), every patch that is named is named exactly 2 times, and one patch is named 2 times in every such block.
All inputs are finite; a program needn't handle non-finite values. No bound on the sum of `bad_pixels` on one device may be relied on, other than what follows from the above.
Results may differ from a plain program's by a relative error of at most 0.0032.
Values may be sent and summed in bfloat16 or wider, within the bound.
A program may use at most 128 MiB of HBM per device.

v0:
```python
import jax
import jax.numpy as jnp
from jax import lax
from jax.sharding import PartitionSpec as P

NBLK = 8
MARGIN = 64
HALF = 10
RIDGE = 0.05


def extended(value, sides, width):
    for axis, dim in sides:
        size, length = (lax.axis_size(axis), value.shape[dim])
        up = [(i, (i + 1) % size) for i in range(size - 1)]
        down = [(j, i) for i, j in up]
        last = lax.slice_in_dim(value, length - width, length, axis=dim)
        leading = lax.slice_in_dim(value, 0, width, axis=dim)
        before = lax.ppermute(last, axis, up)
        after = lax.ppermute(leading, axis, down)
        value = jnp.concatenate([before, value, after], axis=dim)
    return value


def basis_taps():
    spread = jnp.arange(2 * HALF + 1, dtype=jnp.float32)
    scaled = (HALF - spread) / 2.5
    hermite = jnp.stack(
        [
            jnp.ones(scaled.shape, jnp.float32),
            2.0 * scaled,
            4.0 * scaled * scaled - 2.0,
            8.0 * scaled * scaled * scaled - 12.0 * scaled,
        ]
    )
    shaped = hermite * jnp.exp(-0.5 * scaled * scaled)
    shaped = shaped / jnp.sqrt(jnp.sum(shaped * shaped, axis=1, keepdims=True))
    return shaped.astype(jnp.bfloat16)


def solve_normal(system):
    unknowns = system.shape[0]
    rows_index = jnp.arange(unknowns)[:, None, None]
    for column in range(unknowns):
        pivot_row = system[column] / system[column, column][None, :]
        factor = system[:, column, :]
        updated = system - factor[:, None, :] * pivot_row[None, :, :]
        system = jnp.where(rows_index == column, pivot_row[None, :, :], updated)
    return system[:, unknowns, :]


def column_table(profile, block_span, block_width):
    offsets = jnp.arange(block_span)[:, None] - jnp.arange(block_width)[None, :] - (MARGIN - HALF)
    choose = (offsets[None] == jnp.arange(2 * HALF + 1)[:, None, None]).astype(jnp.float32)
    toeplitz = jnp.einsum("at,tnc->nac", profile.astype(jnp.float32), choose)
    return toeplitz.reshape(block_span, 4 * block_width).astype(jnp.bfloat16)


def row_table(profile, strip_rows):
    offsets = jnp.arange(strip_rows + 2 * HALF)[None, :] - jnp.arange(strip_rows)[:, None]
    choose = (offsets[None] == jnp.arange(2 * HALF + 1)[:, None, None]).astype(jnp.float32)
    toeplitz = jnp.einsum("bt,trm->brm", profile.astype(jnp.float32), choose)
    return toeplitz.reshape(4 * strip_rows, strip_rows + 2 * HALF).astype(jnp.bfloat16)


def body(template, science, variance, bad_pixels, intersection_patch, intersection_block):
    profile = basis_taps()
    visit_count, block_count, strip_rows, block_width = science.shape
    device_count = lax.axis_size("visit")
    own_index = lax.axis_index("visit")
    slot_count = visit_count * block_count
    capacity = max(2, -(-slot_count // device_count))
    block_span = block_width + 2 * MARGIN
    padded_rows = strip_rows + 2 * HALF
    all_patch, all_block = (
        lax.all_gather(intersection_patch, "visit", axis=0, tiled=True),
        lax.all_gather(intersection_block, "visit", axis=0, tiled=True),
    )
    source_patch = all_patch.reshape(device_count, slot_count)
    source_block = all_block.reshape(device_count, slot_count)
    slot_index = jnp.arange(slot_count)
    earlier = slot_index[None, :] < slot_index[:, None]
    same_patch = source_patch[:, :, None] == source_patch[:, None, :]
    source_rank = jnp.sum(same_patch & earlier[None], axis=2)
    own_patch = intersection_patch.reshape(slot_count)
    own_rank = lax.dynamic_index_in_dim(source_rank, own_index, 0, keepdims=False)
    own_slot = own_patch * capacity + own_rank
    wanted = (source_patch == own_index)[:, None, :] & (
        source_rank[:, None, :] == jnp.arange(capacity)[None, :, None]
    )
    at_block = source_block[:, :, None] == jnp.arange(NBLK)[None, None, :]
    chooser = jnp.einsum(
        "uck,uko->uco", wanted.astype(jnp.float32), at_block.astype(jnp.float32)
    ).astype(jnp.bfloat16)
    rimmed_strip = extended(template[0], (("template", 0),), HALF)
    strips = lax.all_gather(rimmed_strip[None], "visit", axis=0, tiled=True)
    own_block = intersection_block.reshape(slot_count)

    def cut_block(patch_id, column_block):
        return lax.dynamic_slice(
            strips, (patch_id, 0, column_block * block_width), (1, padded_rows, block_span)
        )[0]

    gathered_blocks = jax.vmap(cut_block)(own_patch, own_block)
    gathered_blocks = gathered_blocks.reshape(visit_count, block_count, padded_rows, block_span)
    across = column_table(profile, block_span, block_width)
    vertical = row_table(profile, strip_rows)
    usable = (1 - bad_pixels).astype(jnp.bfloat16)

    def convolve(inputs):
        blocks, signal, usable_mask = inputs
        smooth = jnp.einsum(
            "jmn,nx->jmx", blocks, across, preferred_element_type=jnp.float32
        ).astype(jnp.bfloat16)
        images = jnp.einsum(
            "ym,jmx->jyx", vertical, smooth, preferred_element_type=jnp.float32
        ).astype(jnp.bfloat16)
        basis_images = images.reshape(block_count, 4, strip_rows, 4, block_width)
        weighted = basis_images * usable_mask[:, None, :, None, :]
        cross_terms = jnp.einsum(
            "jbrac,jdrec->bade", weighted, basis_images, preferred_element_type=jnp.float32
        ).reshape(16, 16)
        with_ones = jnp.einsum(
            "jbrac,jrc->ba", basis_images, usable_mask, preferred_element_type=jnp.float32
        ).reshape(16)
        masked_signal = signal * usable_mask
        with_signal = jnp.einsum(
            "jbrac,jrc->ba", basis_images, masked_signal, preferred_element_type=jnp.float32
        ).reshape(16)
        usable_total = jnp.sum(usable_mask.astype(jnp.float32))
        signal_total = jnp.sum(masked_signal.astype(jnp.float32))
        upper_rows = jnp.concatenate(
            [cross_terms, with_ones[:, None], with_signal[:, None]], axis=1
        )
        bottom = jnp.concatenate([with_ones, usable_total[None], signal_total[None]])[None]
        return (images, jnp.concatenate([upper_rows, bottom], axis=0))

    images_all, partial_sums = lax.map(convolve, (gathered_blocks, science, usable))
    normal = lax.psum(partial_sums, "template")
    ridge_term = RIDGE * (normal[:, 16, 16] + 1.0)
    system = normal + ridge_term[:, None, None] * jnp.eye(17, 18, dtype=jnp.float32)[None]
    fitted = solve_normal(jnp.transpose(system, (1, 2, 0)))

    def differ(inputs):
        images, signal, noise_var, usable_mask, fit_row = inputs
        basis_images = images.reshape(block_count, 4, strip_rows, 4, block_width).astype(
            jnp.float32
        )
        modeled = (
            jnp.einsum(
                "jbrac,ba->jrc",
                basis_images,
                fit_row[:16].reshape(4, 4),
                precision=lax.Precision.HIGHEST,
            )
            + fit_row[16]
        )
        difference = signal.astype(jnp.float32) - modeled
        weight = usable_mask.astype(jnp.float32) / noise_var.astype(jnp.float32)
        return jnp.stack(
            [(weight * difference).astype(jnp.bfloat16), weight.astype(jnp.bfloat16)], axis=1
        )

    payload = lax.map(differ, (images_all, science, variance, usable, fitted.T))
    payload = payload.reshape(slot_count, 2 * strip_rows * block_width)
    placement = (own_slot[None, :] == jnp.arange(device_count * capacity)[:, None]).astype(
        jnp.bfloat16
    )
    outgoing = jnp.einsum(
        "sk,kx->sx", placement, payload, preferred_element_type=jnp.float32
    ).astype(jnp.bfloat16)
    outgoing = outgoing.reshape(device_count, capacity, 2, strip_rows, block_width)
    incoming = lax.all_to_all(outgoing, "visit", split_axis=0, concat_axis=0, tiled=True)
    accumulated = jnp.einsum(
        "uco,ucqrx->oqrx", chooser, incoming, preferred_element_type=jnp.float32
    )
    significance = accumulated[:, 0] / jnp.sqrt(jnp.maximum(accumulated[:, 1], 1.0))
    return significance.transpose(1, 0, 2).reshape(1, strip_rows, NBLK * block_width)


def solution(mesh):
    return jax.shard_map(
        body,
        mesh=mesh,
        in_specs=(
            P("visit", "template", None),
            P("visit", None, "template", None),
            P("visit", None, "template", None),
            P("visit", None, "template", None),
            P("visit", None),
            P("visit", None),
        ),
        out_specs=P("visit", "template", None),
        check_vma=False,
    )
```

profile of v0, /device:TPU:6, one launch (start us, length us, event | category | flops | bytes accessed | tf_op | source)
XLA Modules:
  0.0 547.4 jit_solution(14429271509945404964)
XLA Ops:
  6.5 0.8 slice_bitcast_fusion.1
  7.4 1.9 collective-permute-start
  9.3 3.6 collective-permute-start.1
  13.0 1.6 collective-permute-done.1
  14.6 1.6 maximum_bitcast_fusion.3
  16.5 0.8 fusion.25
  18.5 0.8 copy.311
  19.4 106.7 %all-gather.1 = s32[64,6,4]{1,2,0:T(4,128)S(1)} all-gather(s32[1,6,4]{1,2,0:T(4,128)} %bitcast.457), channel_id=1, replica_groups=mesh['visit'=64,'template'=8] {'visit'}, dimensions={0}, use_global_device_ids=true | all-gather | bytes 6240 | tf_op jit(solution)/shard_map/all_gather | solution.py:76
  126.2 0.7 broadcast_multiply_fusion.1
  127.7 49.8 %all-gather.6.cloned.1.call-done = bf16[64,52,1152]{2,1,0:T(8,128)(2,1)} async-done(((bf16[1,52,1152]{2,1,0:T(8,128)(2,1)}), bf16[64,52,1152]{2,1,0:T(8,128)(2,1)}) %all-gather.6.cloned.1.call-update) | async-done | bytes 7667728 | tf_op jit(solution)/shard_map/all_gather | solution.py:96
  177.5 29.8 %copy.313 = bf16[64,52,1152]{1,0,2:T(8,128)(2,1)} copy(bf16[64,52,1152]{2,1,0:T(8,128)(2,1)} %all-gather.6.cloned.1.call-done) | data formatting | bytes 15335424 | tf_op jit(solution)/shard_map/all_gather | solution.py:96
  207.2 8.5 %gather_fusion = bf16[24,52,256]{1,0,2:T(8,128)(2,1)S(1)} fusion(bf16[64,52,1152]{1,0,2:T(8,128)(2,1)} %copy.313, s32[24]{0:T(128)S(1)} %fusion.71), kind=kCustom, calls=%fused_computation | custom fusion | bytes 1278240 | tf_op jit(solution)/shard_map/vmap()/gather | solution.py:100
  215.8 1.2 copy.315
  217.0 49.1 %while.22 = (s32[]{:T(128)}, bf16[6,4,128,512]{2,3,1,0:T(8,128)(2,1)}, f32[6,17,18]{2,0,1:T(8,128)S(1)}, bf16[6,4,52,256]{3,2,1,0:T(8,128)(2,1)S(1)}, bf16[256,5...) while((s32[]{:T(128)}, ...), condition=%wide.region_5.6_spmd, body=%wide.region_2.5_spmd.sunk | while | flops 91956152 | bytes 9150269 | solution.py:138
  217.0 1.4 bitcast_dynamic-update-slice_fusion.2
  218.8 2.4 fusion.105
  221.3 0.7 convert_reduce_fusion.4
  222.0 1.4 maximum_bitcast_fusion.6
  223.9 0.7 convolution_bitcast_fusion.5
  225.3 1.3 bitcast_dynamic-update-slice_fusion.2
  227.0 2.4 fusion.105
  229.5 0.7 convert_reduce_fusion.4
  230.2 1.4 maximum_bitcast_fusion.6
  233.4 1.3 bitcast_dynamic-update-slice_fusion.2
  235.1 2.4 fusion.105
  237.6 0.7 convert_reduce_fusion.4
  238.3 1.4 maximum_bitcast_fusion.6
  240.2 0.7 convolution_bitcast_fusion.5
  241.6 1.3 bitcast_dynamic-update-slice_fusion.2
  243.3 2.4 fusion.105
  245.8 0.7 convert_reduce_fusion.4
  246.5 1.4 maximum_bitcast_fusion.6
  249.7 1.4 bitcast_dynamic-update-slice_fusion.2
  251.5 2.4 fusion.105
  254.0 0.7 convert_reduce_fusion.4
  254.7 1.4 maximum_bitcast_fusion.6
  257.9 1.4 bitcast_dynamic-update-slice_fusion.2
  259.7 2.4 fusion.105
  262.2 0.7 convert_reduce_fusion.4
  262.9 1.4 maximum_bitcast_fusion.6
  266.1 21.6 %psum.7 = f32[6,17,18]{2,0,1:T(8,128)S(1)} all-reduce(f32[6,17,18]{2,0,1:T(8,128)S(1)} %get-tuple-element.86), channel_id=1, replica_groups=mesh['visit'=64,'template'=8] {'template'}, use_global_device_ids=true, to_apply=%region_6.7 | all-reduce | flops 1836 | bytes 14688 | tf_op jit(solution)/shard_map/psum | solution.py:139
  304.5 30.3 %while.23 = (s32[]{:T(128)}, bf16[6,4,2,32,128]{4,3,2,1,0:T(8,128)(2,1)S(1)}, bf16[6,4,32,128]{3,2,1,0:T(8,128)(2,1)S(1)}, bf16[6,4,32,128]{3,2,1,0:T(8,128)(2,1...) while((s32[]{:T(128)}, ...), condition=%wide.region_8.9_spmd, body=%wide.region_7.8_spmd.sunk | while | flops 3473410 | bytes 4162109 | solution.py:164
  304.6 1.1 constant_dynamic-slice_fusion.4
  307.3 1.4 fusion.109
  308.7 0.8 convert_bitcast_fusion.2
  309.7 1.1 constant_dynamic-slice_fusion.4
  312.3 1.4 fusion.109
  313.7 0.8 convert_bitcast_fusion.2
  314.7 1.1 constant_dynamic-slice_fusion.4
  317.3 1.4 fusion.109
  318.7 0.8 convert_bitcast_fusion.2
  319.7 1.1 constant_dynamic-slice_fusion.4
  322.3 1.4 fusion.109
  323.8 0.8 convert_bitcast_fusion.2
  324.7 1.1 constant_dynamic-slice_fusion.4
  327.3 1.4 fusion.109
  328.8 0.8 convert_bitcast_fusion.2
  329.7 1.1 constant_dynamic-slice_fusion.4
  332.4 1.4 fusion.109
  333.8 0.8 convert_bitcast_fusion.2
  336.3 5.2 copy.354
  341.6 9.5 %all-to-all-start = ((bf16[64,2,2,32,128]{4,1,3,2,0:T(2,128)(2,1)}), bf16[64,2,2,32,128]{4,1,3,2,0:T(2,128)(2,1)S(1)}, u32[]{:S(2)}, u32[]{:S(2)}) async-start(bf16[64,2,2,32,128]{4,1,3,2,0:T(2,128)(2,1)} %copy.354), calls=%async_computation | async-start | bytes 4194304 | tf_op jit(solution)/shard_map/all_to_all | solution.py:173
  351.3 185.8 %all-gather.2 = s32[64,6,4]{1,2,0:T(4,128)S(1)} all-gather(s32[1,6,4]{1,2,0:T(4,128)S(1)} %bitcast.458), channel_id=1, replica_groups=mesh['visit'=64,'template'=8] {'visit'}, dimensions={0}, use_global_device_ids=true | all-gather | bytes 6240 | tf_op jit(solution)/shard_map/all_gather | solution.py:77
  537.5 2.3 fusion.26
  (284 shorter events, 43.9 us)
Async XLA Ops:
  6.5 121.1 %copy-start.1 = (s32[6,4,32,128]{3,2,1,0:T(8,128)S(1)}, s32[6,4,32,128]{3,2,1,0:T(8,128)}, u32[]{:S(2)}) copy-start(s32[6,4,32,128]{3,2,1,0:T(8,128)} %param.13) | copy-start | bytes 1179652
  6.5 170.9 %all-gather.6.cloned.1.call-start = ((), (), s32[]{:S(2)}) async-start(), calls=%async_computation.1 | async-start | bytes 8386560 | tf_op jit(solution)/shard_map/all_gather | solution.py:96
  7.4 5.6 %collective-permute-start = (bf16[10,1152]{1,0:T(8,128)(2,1)S(1)}, bf16[10,1152]{1,0:T(8,128)(2,1)S(1)}, u32[]{:S(2)}, u32[]{:S(2)}) collective-permute-start(bf16[10,1152]{1,0:T(8,128)(2,1)S(1)} %get-tuple-element.214), channel_id=1, source_target_pairs={{0,1},{1,2},{2,3},{3,4},{4,5},{5,6},{6,7},{8,9},{9,10},{10,11},{11... | collective-permute-start | bytes 69128 | tf_op jit(solution)/shard_map/ppermute | solution.py:19
  9.3 5.3 collective-permute-start.1
  207.2 9.8 %copy-start = (bf16[6,4,32,128]{3,2,1,0:T(8,128)(2,1)S(1)}, bf16[6,4,32,128]{3,2,1,0:T(8,128)(2,1)}, u32[]{:S(2)}) copy-start(bf16[6,4,32,128]{3,2,1,0:T(8,128)(2,1)} %param.11) | copy-start | bytes 589828
  341.6 9.7 %copy-start.2 = (s32[6,4]{0,1:T(4,128)S(1)}, s32[6,4]{0,1:T(4,128)}, u32[]{:S(2)}) copy-start(s32[6,4]{0,1:T(4,128)} %param.15) | copy-start | bytes 292
  341.6 196.0 %all-to-all-start = ((bf16[64,2,2,32,128]{4,1,3,2,0:T(2,128)(2,1)}), bf16[64,2,2,32,128]{4,1,3,2,0:T(2,128)(2,1)S(1)}, u32[]{:S(2)}, u32[]{:S(2)}) async-start(bf16[64,2,2,32,128]{4,1,3,2,0:T(2,128)(2,1)} %copy.354), calls=%async_computation | async-start | bytes 4194304 | tf_op jit(solution)/shard_map/all_to_all | solution.py:173
Sparse Core Ops, SparseCore 0:
  16.3 161.1 all-gather.5
where the time goes:
time: 549 us; the launch traced here: 547 us
  blocking collectives  314 us (57%)
  local copies, waits for them, and re-layouts  75.3 us (14%)
  waiting for transfers between devices  51.4 us (9%)
  other arithmetic  39.7 us (7%)
  matrix products  36.9 us (7%)
  starting transfers between devices  15.1 us (3%)
  between operations  13.9 us (3%)
    all_gather x1, blocking collectives, body(): lax.all_gather(intersection_block, 'visit', axis=0, tiled=True)  186 us
    all_gather x1, blocking collectives, body(): lax.all_gather(intersection_patch, 'visit', axis=0, tiled=True)  107 us
    all_gather x1, waiting for transfers between devices, body(): strips = lax.all_gather(rimmed_strip[None], 'visit', axis=0, tiled=True)  49.8 us
    all_gather x1, local copies, waits for them, and re-layouts, body(): strips = lax.all_gather(rimmed_strip[None], 'visit', axis=0, tiled=True)  29.8 us
    psum x1, blocking collectives, body(): normal = lax.psum(partial_sums, 'template')  21.6 us
    dot_general x6, matrix products, convolve(): jnp.einsum('jbrac,jrc->ba', basis_images, usable_mask, preferred_element_...  14.3 us
  transfers between devices with their start and end apart: 4, of which 2 were waited for; matrix products, arithmetic and copies ran while one was open for 1% of the time, Pallas kernels for 0%

commit v1 on v0

--- a/solution.py
+++ b/solution.py
@@ -7,6 +7,13 @@
 MARGIN = 64
 HALF = 10
 RIDGE = 0.05
+
+
+def swapped_in(array, axis, dim):
+    n_dev = lax.axis_size(axis)
+    pieces = jnp.stack([array for _ in range(n_dev)])
+    pieces = lax.all_to_all(pieces, axis, split_axis=0, concat_axis=0)
+    return jnp.concatenate(pieces, axis=dim)
 
 
 def extended(value, sides, width):
@@ -73,7 +80,7 @@
     block_span = block_width + 2 * MARGIN
     padded_rows = strip_rows + 2 * HALF
     all_patch, all_block = (
-        lax.all_gather(intersection_patch, "visit", axis=0, tiled=True),
+        swapped_in(intersection_patch, "visit", 0),
         lax.all_gather(intersection_block, "visit", axis=0, tiled=True),
     )
     source_patch = all_patch.reshape(device_count, slot_count)

time: 549 us -> 550 us (level)
  blocking collectives: 314 us -> 208 us
  waiting for transfers between devices: 51.4 us -> 137 us
  starting transfers between devices: 15.1 us -> 33.8 us
    all_gather x1 -> x0, blocking collectives: 107 us -> none  [body(): lax.all_gather(intersection_patch, 'visit', axis=0, tiled=True)]
    all_gather x1, waiting for transfers between devices: 49.8 us -> 125 us  [body(): strips = lax.all_gather(rimmed_strip[None], 'visit', axis=0, tiled=True)]
    all_to_all x0 -> x1, starting transfers between devices: none -> 18.7 us  [swapped_in(): pieces = lax.all_to_all(pieces, axis, split_axis=0, concat_axis=0)]
    all_to_all x0 -> x1, waiting for transfers between devices: none -> 11 us  [swapped_in(): pieces = lax.all_to_all(pieces, axis, split_axis=0, concat_axis=0)]
  transfers between devices with their start and end apart: 4 -> 5, of which waited for: 2 -> 3; matrix products, arithmetic and copies ran while one was open for 1% -> 1% of each run, Pallas kernels for 0% -> 0%
where the time goes in v1:
time: 550 us; the launch traced here: 548 us
  blocking collectives  208 us (38%)
  waiting for transfers between devices  137 us (25%)
  local copies, waits for them, and re-layouts  76.6 us (14%)
  other arithmetic  40.6 us (7%)
  matrix products  36.9 us (7%)
  starting transfers between devices  33.8 us (6%)
  between operations  13.9 us (3%)
    all_gather x1, blocking collectives, body(): lax.all_gather(intersection_block, 'visit', axis=0, tiled=True)  186 us
    all_gather x1, waiting for transfers between devices, body(): strips = lax.all_gather(rimmed_strip[None], 'visit', axis=0, tiled=True)  125 us
    all_gather x1, local copies, waits for them, and re-layouts, body(): strips = lax.all_gather(rimmed_strip[None], 'visit', axis=0, tiled=True)  29.8 us
    psum x1, blocking collectives, body(): normal = lax.psum(partial_sums, 'template')  21.5 us
    all_to_all x1, starting transfers between devices, swapped_in(): pieces = lax.all_to_all(pieces, axis, split_axis=0, concat_axis=0)  18.7 us
    dot_general x6, matrix products, convolve(): jnp.einsum('jbrac,jrc->ba', basis_images, usable_mask, preferred_element_...  14.3 us
  transfers between devices with their start and end apart: 5, of which 3 were waited for; matrix products, arithmetic and copies ran while one was open for 1% of the time, Pallas kernels for 0%

profile of v1, /device:TPU:6, one launch (start us, length us, event | category | flops | bytes accessed | tf_op | source)
XLA Modules:
  0.0 547.9 jit_solution(9077385758904027652)
XLA Ops:
  6.5 0.8 slice_bitcast_fusion.1
  7.3 1.9 collective-permute-start
  9.3 3.6 collective-permute-start.1
  12.9 1.6 collective-permute-done.1
  14.5 1.6 maximum_bitcast_fusion.3
  16.1 1.4 stack.8
  17.5 18.7 %all-to-all-start = ((s32[64,6,4]{1,2,0:T(4,128)}), s32[64,6,4]{1,2,0:T(4,128)S(1)}, u32[]{:S(2)}, u32[]{:S(2)}) async-start(s32[64,6,4]{1,2,0:T(4,128)} %stack.8), calls=%async_computation | async-start | bytes 262144 | tf_op jit(solution)/shard_map/all_to_all | solution.py:15
  36.2 0.8 copy.374
  39.3 0.8 fusion.25
  40.1 1.0 subtract_convert_fusion
  41.5 11.0 %all-to-all-done = s32[64,6,4]{1,2,0:T(4,128)S(1)} async-done(((s32[64,6,4]{1,2,0:T(4,128)}), s32[64,6,4]{1,2,0:T(4,128)S(1)}, u32[]{:S(2)}, u32[]{:S(2)}) %all-to-all-start) | async-done | bytes 6176 | tf_op jit(solution)/shard_map/all_to_all | solution.py:15
  53.0 124.8 %all-gather.5.cloned.1.call-done = bf16[64,52,1152]{2,1,0:T(8,128)(2,1)} async-done(((bf16[1,52,1152]{2,1,0:T(8,128)(2,1)}), bf16[64,52,1152]{2,1,0:T(8,128)(2,1)}) %all-gather.5.cloned.1.call-update) | async-done | bytes 7667728 | tf_op jit(solution)/shard_map/all_gather | solution.py:103
  177.8 29.8 %copy.376 = bf16[64,52,1152]{1,0,2:T(8,128)(2,1)} copy(bf16[64,52,1152]{2,1,0:T(8,128)(2,1)} %all-gather.5.cloned.1.call-done) | data formatting | bytes 15335424 | tf_op jit(solution)/shard_map/all_gather | solution.py:103
  207.6 8.5 %gather_fusion = bf16[24,52,256]{1,0,2:T(8,128)(2,1)S(1)} fusion(bf16[64,52,1152]{1,0,2:T(8,128)(2,1)} %copy.376, s32[24]{0:T(128)S(1)} %fusion.71), kind=kCustom, calls=%fused_computation | custom fusion | bytes 1278240 | tf_op jit(solution)/shard_map/vmap()/gather | solution.py:107
  216.1 1.2 copy.378
  217.4 49.1 %while.22 = (s32[]{:T(128)}, bf16[6,4,128,512]{2,3,1,0:T(8,128)(2,1)}, f32[6,17,18]{2,0,1:T(8,128)S(1)}, bf16[6,4,52,256]{3,2,1,0:T(8,128)(2,1)S(1)}, bf16[256,5...) while((s32[]{:T(128)}, ...), condition=%wide.region_5.6_spmd, body=%wide.region_2.5_spmd.sunk | while | flops 91956152 | bytes 9150269 | solution.py:145
  217.4 1.4 bitcast_dynamic-update-slice_fusion.2
  219.1 2.4 fusion.105
  221.6 0.7 convert_reduce_fusion.4
  222.3 1.4 maximum_bitcast_fusion.6
  225.6 1.3 bitcast_dynamic-update-slice_fusion.2
  227.3 2.4 fusion.105
  229.8 0.7 convert_reduce_fusion.4
  230.5 1.4 maximum_bitcast_fusion.6
  233.8 1.3 bitcast_dynamic-update-slice_fusion.2
  235.5 2.4 fusion.105
  238.0 0.7 convert_reduce_fusion.4
  238.7 1.4 maximum_bitcast_fusion.6
  241.9 1.3 bitcast_dynamic-update-slice_fusion.2
  243.6 2.4 fusion.105
  246.1 0.7 convert_reduce_fusion.4
  246.8 1.4 maximum_bitcast_fusion.6
  250.1 1.4 bitcast_dynamic-update-slice_fusion.2
  251.8 2.4 fusion.105
  254.3 0.7 convert_reduce_fusion.4
  255.0 1.4 maximum_bitcast_fusion.6
  258.3 1.4 bitcast_dynamic-update-slice_fusion.2
  260.1 2.4 fusion.105
  262.6 0.7 convert_reduce_fusion.4
  263.3 1.4 maximum_bitcast_fusion.6
  266.5 21.5 %psum.7 = f32[6,17,18]{2,0,1:T(8,128)S(1)} all-reduce(f32[6,17,18]{2,0,1:T(8,128)S(1)} %get-tuple-element.86), channel_id=1, replica_groups=mesh['visit'=64,'template'=8] {'template'}, use_global_device_ids=true, to_apply=%region_6.7 | all-reduce | flops 1836 | bytes 14688 | tf_op jit(solution)/shard_map/psum | solution.py:146
  304.8 30.3 %while.23 = (s32[]{:T(128)}, bf16[6,4,2,32,128]{4,3,2,1,0:T(8,128)(2,1)S(1)}, bf16[6,4,32,128]{3,2,1,0:T(8,128)(2,1)S(1)}, bf16[6,4,32,128]{3,2,1,0:T(8,128)(2,1...) while((s32[]{:T(128)}, ...), condition=%wide.region_8.9_spmd, body=%wide.region_7.8_spmd.sunk | while | flops 3473410 | bytes 4162109 | solution.py:171
  305.0 1.1 constant_dynamic-slice_fusion.4
  307.6 1.4 fusion.109
  309.0 0.8 convert_bitcast_fusion.2
  310.0 1.1 constant_dynamic-slice_fusion.4
  312.6 1.4 fusion.109
  314.0 0.8 convert_bitcast_fusion.2
  315.0 1.1 constant_dynamic-slice_fusion.4
  317.6 1.4 fusion.109
  319.1 0.8 convert_bitcast_fusion.2
  320.0 1.1 constant_dynamic-slice_fusion.4
  322.7 1.4 fusion.109
  324.1 0.8 convert_bitcast_fusion.2
  325.0 1.1 constant_dynamic-slice_fusion.4
  327.7 1.4 fusion.109
  329.1 0.8 convert_bitcast_fusion.2
  330.1 1.1 constant_dynamic-slice_fusion.4
  332.7 1.4 fusion.109
  334.1 0.8 convert_bitcast_fusion.2
  336.6 5.2 copy.417
  341.9 9.5 %all-to-all-start.1 = ((bf16[64,2,2,32,128]{4,1,3,2,0:T(2,128)(2,1)}), bf16[64,2,2,32,128]{4,1,3,2,0:T(2,128)(2,1)S(1)}, u32[]{:S(2)}, u32[]{:S(2)}) async-start(bf16[64,2,2,32,128]{4,1,3,2,0:T(2,128)(2,1)} %copy.417), calls=%async_computation.1 | async-start | bytes 4194304 | tf_op jit(solution)/shard_map/all_to_all | solution.py:180
  351.4 186.0 %all-gather.1 = s32[64,6,4]{1,2,0:T(4,128)S(1)} all-gather(s32[1,6,4]{1,2,0:T(4,128)S(1)} %bitcast.456), channel_id=1, replica_groups=mesh['visit'=64,'template'=8] {'visit'}, dimensions={0}, use_global_device_ids=true | all-gather | bytes 6240 | tf_op jit(solution)/shard_map/all_gather | solution.py:84
  538.1 2.3 fusion.26
  (284 shorter events, 45.9 us)
Async XLA Ops:
  6.5 171.2 %all-gather.5.cloned.1.call-start = ((), (), s32[]{:S(2)}) async-start(), calls=%async_computation.2 | async-start | bytes 8386560 | tf_op jit(solution)/shard_map/all_gather | solution.py:103
  7.3 5.6 %collective-permute-start = (bf16[10,1152]{1,0:T(8,128)(2,1)S(1)}, bf16[10,1152]{1,0:T(8,128)(2,1)S(1)}, u32[]{:S(2)}, u32[]{:S(2)}) collective-permute-start(bf16[10,1152]{1,0:T(8,128)(2,1)S(1)} %get-tuple-element.229), channel_id=1, source_target_pairs={{0,1},{1,2},{2,3},{3,4},{4,5},{5,6},{6,7},{8,9},{9,10},{10,11},{11... | collective-permute-start | bytes 69128 | tf_op jit(solution)/shard_map/ppermute | solution.py:26
  9.3 5.3 collective-permute-start.1
  17.5 35.0 %all-to-all-start = ((s32[64,6,4]{1,2,0:T(4,128)}), s32[64,6,4]{1,2,0:T(4,128)S(1)}, u32[]{:S(2)}, u32[]{:S(2)}) async-start(s32[64,6,4]{1,2,0:T(4,128)} %stack.8), calls=%async_computation | async-start | bytes 262144 | tf_op jit(solution)/shard_map/all_to_all | solution.py:15
  207.6 9.8 %copy-start = (bf16[6,4,32,128]{3,2,1,0:T(8,128)(2,1)S(1)}, bf16[6,4,32,128]{3,2,1,0:T(8,128)(2,1)}, u32[]{:S(2)}) copy-start(bf16[6,4,32,128]{3,2,1,0:T(8,128)(2,1)} %param.11) | copy-start | bytes 589828
  341.9 9.5 %copy-start.1 = (s32[6,4]{0,1:T(4,128)S(1)}, s32[6,4]{0,1:T(4,128)}, u32[]{:S(2)}) copy-start(s32[6,4]{0,1:T(4,128)} %param.15) | copy-start | bytes 292
  341.9 196.2 %all-to-all-start.1 = ((bf16[64,2,2,32,128]{4,1,3,2,0:T(2,128)(2,1)}), bf16[64,2,2,32,128]{4,1,3,2,0:T(2,128)(2,1)S(1)}, u32[]{:S(2)}, u32[]{:S(2)}) async-start(bf16[64,2,2,32,128]{4,1,3,2,0:T(2,128)(2,1)} %copy.417), calls=%async_computation.1 | async-start | bytes 4194304 | tf_op jit(solution)/shard_map/all_to_all | solution.py:180
Sparse Core Ops, SparseCore 0:
  16.2 161.4 all-gather.4
